TPU v7x, 32 devices: a whole 2x2x4 slice. The times are simulated.
32 devices in a mesh: fsdp: 4 (over y, core), ctx: 4 (over z), uly: 2 (over x).
Axes of the slice: x: 2, y: 2, z: 4, core: 2. Of those that a mesh axis runs over, the one named last changes fastest.
Arguments:
- query_states: bfloat16 [12, 384, 8192], P('fsdp', 'ctx', 'uly'), may hold values from -8 to 8
- key_projections: bfloat16 [12, 384, 1024], P('fsdp', 'ctx', 'uly'), may hold values from -8 to 8
- value_projections: bfloat16 [12, 384, 1024], P('fsdp', 'ctx', 'uly'), may hold values from -6 to 6
- layer_bias: bfloat16 [10240], P('fsdp'), may hold values from -3 to 3
- positions: int32 [12, 384], P('fsdp', 'ctx'), may hold values from 0 to 383, as said below
- rescale: float32 [2, 64], replicated, may hold values from 1 to 16
- table_index: int32 [12], P('fsdp'), may hold values from 0 to 1
Outputs:
- attended: bfloat16 [12, 384, 8192], P('fsdp', 'ctx', 'uly')
Inputs may be any that keep to these rules, and one draw needn't show every extreme that they name: In each sequence the rows come in aligned runs of 48; every run holds 48 consecutive positions in increasing order, starting at a multiple of 48, and every position 0 to 383 occurs once. The order of the runs differs between sequences.
All inputs are finite; a program needn't handle non-finite values.
Results may differ from a plain program's by a relative error of at most 0.012.
Values may be sent and summed in bfloat16 or wider, within the bound.
A program may use at most 64 MiB of HBM per device.

v0:
```python
import math
import jax
import jax.numpy as jnp
from jax import lax
from jax.sharding import PartitionSpec as P

QUERY_HEADS = 64
KEY_VALUE_HEADS = 8
HEAD_SIZE = 128
rope_base = 1000000.0
masked_value = -1e30


def apply_rotation(states, positions, scale_factors):
    half_dim = states.shape[-1] // 2
    exponent = jnp.arange(half_dim, dtype=jnp.float32) * (2.0 / states.shape[-1])
    inverse = 1.0 / (scale_factors * jnp.power(jnp.float32(rope_base), exponent)[None, :])
    angles = positions.astype(jnp.float32)[:, :, None] * inverse[:, None, :]
    cosine = jnp.cos(angles)[:, :, None, :]
    sine_wave = jnp.sin(angles)[:, :, None, :]
    leading = states[..., :half_dim]
    trailing = states[..., half_dim:]
    return jnp.concatenate(
        [leading * cosine - trailing * sine_wave, trailing * cosine + leading * sine_wave], axis=-1
    )


def make_folder(query_grouped, query_positions, key_heads_here):

    def attend(running, block_piece):
        highest, totals, weighted_blend = running
        block_keys, block_values, block_positions = block_piece
        key_rows = block_keys.reshape(-1, key_heads_here, HEAD_SIZE)
        value_rows = block_values.reshape(-1, key_heads_here, HEAD_SIZE)
        scores = jnp.einsum(
            "qgrd,kgd->grqk", query_grouped, key_rows, preferred_element_type=jnp.float32
        ) / math.sqrt(HEAD_SIZE)
        allowed = block_positions[0][None, :] <= query_positions[0][:, None]
        block_high = jnp.max(jnp.where(allowed, scores, masked_value), axis=-1)
        new_high = jnp.maximum(highest, block_high)
        weights = jnp.where(allowed, jnp.exp(scores - new_high[..., None]), 0.0)
        shrink = jnp.exp(highest - new_high)
        totals = jnp.sum(weights, axis=-1)
        weighted_blend = jnp.einsum(
            "grqk,kgd->grqd",
            weights.astype(jnp.bfloat16),
            value_rows,
            preferred_element_type=jnp.float32,
        )
        return (new_high, totals, weighted_blend)

    def folder(running, block_piece, offset):
        return attend(running, block_piece)

    return folder


def initial_state(key_heads_here, group_fraction, query_rows):
    return (
        jnp.full((key_heads_here, group_fraction, query_rows), masked_value, jnp.float32),
        jnp.zeros((key_heads_here, group_fraction, query_rows), jnp.float32),
        jnp.zeros((key_heads_here, group_fraction, query_rows, HEAD_SIZE), jnp.float32),
    )


def finish(running, query_rows):
    highest, totals, weighted_blend = running
    normalized = weighted_blend / totals[..., None]
    return normalized.transpose(2, 0, 1, 3).reshape(1, query_rows, -1).astype(jnp.bfloat16)


def on_device(
    query_states, key_projections, value_projections, layer_bias, positions, rescale, table_index
):
    bias_terms = lax.all_gather(layer_bias, "fsdp", axis=0, tiled=True).astype(jnp.float32)
    local_count = query_states.shape[0]
    tokens_here = query_states.shape[1]
    query_heads_here = query_states.shape[2] // HEAD_SIZE
    key_heads_here = key_projections.shape[2] // HEAD_SIZE
    uly_place = lax.axis_index("uly")
    query_span_width = QUERY_HEADS * HEAD_SIZE
    key_span_width = KEY_VALUE_HEADS * HEAD_SIZE
    query_bias = lax.dynamic_slice_in_dim(
        bias_terms[:query_span_width].reshape(QUERY_HEADS, HEAD_SIZE),
        uly_place * query_heads_here,
        query_heads_here,
        0,
    )
    key_offset_bias = lax.dynamic_slice_in_dim(
        bias_terms[query_span_width : query_span_width + key_span_width].reshape(
            KEY_VALUE_HEADS, HEAD_SIZE
        ),
        uly_place * key_heads_here,
        key_heads_here,
        0,
    )
    value_offset_bias = lax.dynamic_slice_in_dim(
        bias_terms[query_span_width + key_span_width :].reshape(KEY_VALUE_HEADS, HEAD_SIZE),
        uly_place * key_heads_here,
        key_heads_here,
        0,
    )
    selector = (
        jnp.arange(rescale.shape[0], dtype=jnp.int32)[None, :] == table_index[:, None]
    ).astype(jnp.float32)
    scale_factors = jnp.dot(selector, rescale, precision=lax.Precision.HIGHEST)
    query_rotated_all = apply_rotation(
        query_states.astype(jnp.float32).reshape(
            local_count, tokens_here, query_heads_here, HEAD_SIZE
        )
        + query_bias,
        positions,
        scale_factors,
    )
    query_rotated_all = query_rotated_all.astype(jnp.bfloat16).reshape(
        local_count, tokens_here, query_heads_here * HEAD_SIZE
    )
    key_rotated_all = apply_rotation(
        key_projections.astype(jnp.float32).reshape(
            local_count, tokens_here, key_heads_here, HEAD_SIZE
        )
        + key_offset_bias,
        positions,
        scale_factors,
    )
    key_rotated_all = key_rotated_all.astype(jnp.bfloat16).reshape(
        local_count, tokens_here, key_heads_here * HEAD_SIZE
    )
    value_all = (
        value_projections.astype(jnp.float32).reshape(
            local_count, tokens_here, key_heads_here, HEAD_SIZE
        )
        + value_offset_bias
    ).astype(jnp.bfloat16)
    value_all = value_all.reshape(local_count, tokens_here, key_heads_here * HEAD_SIZE)
    group_fraction = QUERY_HEADS // KEY_VALUE_HEADS
    results = []
    for member in range(local_count):
        query_rotated_rows = query_rotated_all[member : member + 1]
        key_rotated_rows = key_rotated_all[member : member + 1]
        value_with_bias = value_all[member : member + 1]
        member_positions = positions[member : member + 1]
        query_grouped = query_rotated_rows.reshape(
            tokens_here, key_heads_here, group_fraction, HEAD_SIZE
        )
        folder = make_folder(query_grouped, member_positions, key_heads_here)
        running = folder(
            initial_state(key_heads_here, group_fraction, tokens_here),
            (
                lax.all_gather(key_rotated_rows, "ctx", axis=1, tiled=True),
                lax.all_gather(value_with_bias, "ctx", axis=1, tiled=True),
                lax.all_gather(member_positions, "ctx", axis=1, tiled=True),
            ),
            jnp.int32(0),
        )
        results.append(finish(running, tokens_here))
    return jnp.concatenate(results, axis=0)


def solution(mesh):
    in_specs = (
        P("fsdp", "ctx", "uly"),
        P("fsdp", "ctx", "uly"),
        P("fsdp", "ctx", "uly"),
        P("fsdp"),
        P("fsdp", "ctx"),
        P(),
        P("fsdp"),
    )
    out_specs = P("fsdp", "ctx", "uly")
    return jax.shard_map(
        on_device, mesh=mesh, in_specs=in_specs, out_specs=out_specs, check_vma=False
    )
```

profile of v0, /device:TPU:0, one launch (start us, length us, event | category | flops | bytes accessed | tf_op | source)
XLA Modules:
  0.0 148.7 jit_solution(562633976710418100)
XLA Ops:
  0.9 6.2 %all-gather = bf16[4,1,2560]{2,1,0:T(2,128)(2,1)S(1)} all-gather(bf16[1,1,2560]{2,1,0:T(2,128)(2,1)S(1)} %reshape.188), channel_id=1, replica_groups=mesh['fsdp'=4,'ctx'=4,'uly'=2] {'fsdp'}, dimensions={0}, use_global_device_ids=true | all-gather | bytes 25600 | tf_op jit(solution)/shard_map/all_gather | solution.py:75
  8.4 1.1 reshape.174
  13.4 15.4 %all_gather.32 = bf16[1,384,512]{2,1,0:T(8,128)(2,1)S(1)} all-gather(bf16[1,96,512]{2,1,0:T(8,128)(2,1)S(1)} %slice.114), channel_id=1, replica_groups=mesh['fsdp'=4,'ctx'=4,'uly'=2] {'ctx'}, dimensions={1}, use_global_device_ids=true | all-gather | bytes 491520 | tf_op jit(solution)/shard_map/all_gather | solution.py:150
  30.4 1.7 %subtract_convert_fusion = (bf16[3,96,32,64]{3,1,2,0:T(8,128)(2,1)S(1)}, bf16[3,96,32,64]{3,1,2,0:T(8,128)(2,1)S(1)}) fusion(f32[3,96,32,128]{3,1,2,0:T(8,128)S(1)} %bitcast_add_fusion, f32[3,96,64]{2,1,0:T(8,128)S(1)} %get-tuple-element.24, f32[3,96,64]{2,1,0:T(8,128)S(1)} %get-tuple-element.23), kind=kLoop, calls=%fused_computation.18 | loop fusion | flops 4718592 | bytes 7225344 | tf_op jit(solution)/shard_map/convert.3
  32.1 1.3 fusion.44
  35.0 9.2 %all-reduce.3 = (s32[384]{0:T(512)}, s32[384]{0:T(512)}, s32[384]{0:T(512)S(1)}) all-reduce(s32[384]{0:T(512)S(1)} %fusion.56, s32[384]{0:T(512)S(1)} %fusion.55, s32[384]{0:T(512)S(1)} %fusion.54), channel_id=1, replica_groups=mesh['fsdp'=4,'ctx'=4,'uly'=2] {'ctx'}, use_global_device_ids=true, to_apply=%add.2 | all-reduce | flops 1152 | bytes 9216
  44.3 1.0 fusion.6
  45.3 2.1 %copy-done.1 = f32[4,384,96,8]{1,2,3,0:T(8,128)} copy-done((f32[4,384,96,8]{1,2,3,0:T(8,128)}, f32[4,384,96,8]{1,2,3,0:T(8,128)S(1)}, u32[]{:S(2)}) %copy-start.1) | copy-done | bytes 4718616
  47.5 1.6 %fusion.9 = f32[4,8,96]{2,1,0:T(8,128)S(1)} fusion(f32[4,384,96,8]{1,2,3,0:T(8,128)S(1)} %get-tuple-element.33, f32[4,8,96]{2,1,0:T(8,128)S(1)} %broadcast_maximum_fusion.2, pred[96,384]{1,0:T(8,128)(4,1)S(1)} %broadcast_compare_fusion.2), kind=kLoop, calls=%fused_computation.19 | loop fusion | flops 4715520 | bytes 4780032 | tf_op jit(solution)/shard_map/reduce_sum | solution.py:43
  49.5 15.1 %all_gather.33 = bf16[1,384,512]{2,1,0:T(8,128)(2,1)S(1)} all-gather(bf16[1,96,512]{2,1,0:T(8,128)(2,1)S(1)} %slice.123), channel_id=1, replica_groups=mesh['fsdp'=4,'ctx'=4,'uly'=2] {'ctx'}, dimensions={1}, use_global_device_ids=true | all-gather | bytes 491520 | tf_op jit(solution)/shard_map/all_gather | solution.py:151
  64.9 3.7 %fusion.35 = bf16[96,4,8,128]{3,0,2,1:T(8,128)(2,1)S(1)} fusion(bf16[384,4,128,1]{0,2,3,1:T(8,128)(2,1)S(1)} %bitcast.148, f32[4,384,96,8]{1,2,3,0:T(8,128)} %copy-done.1, f32[4,8,96]{2,1,0:T(8,128)S(1)} %broadcast_maximum_fusion.2, pred[96,384]{1,0:T(8,128)(4,1)S(1)} %broadcast_compare_fusion.2, f32[96,4,8]{0,2,1:T(8,128)S(1)} %bitcast.151), kind=kOutput, calls=%fused_computation.50 | convolution fusion | flops 307494912 | bytes 5959680 | tf_op jit(solution)/shard_map/grqk,kgd->grqd/dot_general | solution.py:44
  69.3 14.4 %all_gather.35 = bf16[1,384,512]{2,1,0:T(8,128)(2,1)S(1)} all-gather(bf16[1,96,512]{2,1,0:T(8,128)(2,1)S(1)} %slice.126), channel_id=1, replica_groups=mesh['fsdp'=4,'ctx'=4,'uly'=2] {'ctx'}, dimensions={1}, use_global_device_ids=true | all-gather | bytes 491520 | tf_op jit(solution)/shard_map/all_gather | solution.py:150
  84.1 1.0 fusion.3
  85.1 2.1 %copy-done.3 = f32[4,384,96,8]{1,2,3,0:T(8,128)} copy-done((f32[4,384,96,8]{1,2,3,0:T(8,128)}, f32[4,384,96,8]{1,2,3,0:T(8,128)S(1)}, u32[]{:S(2)}) %copy-start.3) | copy-done | bytes 4718616
  87.2 1.6 %fusion.11 = f32[4,8,96]{2,1,0:T(8,128)S(1)} fusion(f32[4,384,96,8]{1,2,3,0:T(8,128)S(1)} %get-tuple-element.31, f32[4,8,96]{2,1,0:T(8,128)S(1)} %broadcast_maximum_fusion.1, pred[96,384]{1,0:T(8,128)(4,1)S(1)} %broadcast_compare_fusion.1), kind=kLoop, calls=%fused_computation.21 | loop fusion | flops 4715520 | bytes 4780032 | tf_op jit(solution)/shard_map/reduce_sum | solution.py:43
  88.9 14.4 %all_gather.36 = bf16[1,384,512]{2,1,0:T(8,128)(2,1)S(1)} all-gather(bf16[1,96,512]{2,1,0:T(8,128)(2,1)S(1)} %slice.129), channel_id=1, replica_groups=mesh['fsdp'=4,'ctx'=4,'uly'=2] {'ctx'}, dimensions={1}, use_global_device_ids=true | all-gather | bytes 491520 | tf_op jit(solution)/shard_map/all_gather | solution.py:151
  103.5 3.7 %fusion.34 = bf16[96,4,8,128]{3,0,2,1:T(8,128)(2,1)S(1)} fusion(bf16[384,4,128,1]{0,2,3,1:T(8,128)(2,1)S(1)} %bitcast.149, f32[4,384,96,8]{1,2,3,0:T(8,128)} %copy-done.3, f32[4,8,96]{2,1,0:T(8,128)S(1)} %broadcast_maximum_fusion.1, pred[96,384]{1,0:T(8,128)(4,1)S(1)} %broadcast_compare_fusion.1, f32[96,4,8]{0,2,1:T(8,128)S(1)} %bitcast.153), kind=kOutput, calls=%fused_computation.48 | convolution fusion | flops 307494912 | bytes 5959680 | tf_op jit(solution)/shard_map/grqk,kgd->grqd/dot_general | solution.py:44
  107.9 15.1 %all_gather.38 = bf16[1,384,512]{2,1,0:T(8,128)(2,1)S(1)} all-gather(bf16[1,96,512]{2,1,0:T(8,128)(2,1)S(1)} %slice.132), channel_id=1, replica_groups=mesh['fsdp'=4,'ctx'=4,'uly'=2] {'ctx'}, dimensions={1}, use_global_device_ids=true | all-gather | bytes 491520 | tf_op jit(solution)/shard_map/all_gather | solution.py:150
  123.4 1.0 fusion
  124.4 2.1 %copy-done.2 = f32[4,384,96,8]{1,2,3,0:T(8,128)} copy-done((f32[4,384,96,8]{1,2,3,0:T(8,128)}, f32[4,384,96,8]{1,2,3,0:T(8,128)S(1)}, u32[]{:S(2)}) %copy-start.2) | copy-done | bytes 4718616
  126.5 1.6 %fusion.13 = f32[4,8,96]{2,1,0:T(8,128)S(1)} fusion(f32[4,384,96,8]{1,2,3,0:T(8,128)S(1)} %get-tuple-element.29, f32[4,8,96]{2,1,0:T(8,128)S(1)} %broadcast_maximum_fusion, pred[96,384]{1,0:T(8,128)(4,1)S(1)} %broadcast_compare_fusion), kind=kLoop, calls=%fused_computation.23 | loop fusion | flops 4715520 | bytes 4780032 | tf_op jit(solution)/shard_map/reduce_sum | solution.py:43
  128.2 14.3 %all_gather.39 = bf16[1,384,512]{2,1,0:T(8,128)(2,1)S(1)} all-gather(bf16[1,96,512]{2,1,0:T(8,128)(2,1)S(1)} %slice.135), channel_id=1, replica_groups=mesh['fsdp'=4,'ctx'=4,'uly'=2] {'ctx'}, dimensions={1}, use_global_device_ids=true | all-gather | bytes 491520 | tf_op jit(solution)/shard_map/all_gather | solution.py:151
  142.7 3.7 %fusion.33 = bf16[96,4,8,128]{3,0,2,1:T(8,128)(2,1)S(1)} fusion(bf16[384,4,128,1]{0,2,3,1:T(8,128)(2,1)S(1)} %bitcast.150, f32[4,384,96,8]{1,2,3,0:T(8,128)} %copy-done.2, f32[4,8,96]{2,1,0:T(8,128)S(1)} %broadcast_maximum_fusion, pred[96,384]{1,0:T(8,128)(4,1)S(1)} %broadcast_compare_fusion, f32[96,4,8]{0,2,1:T(8,128)S(1)} %bitcast.152), kind=kOutput, calls=%fused_computation.46 | convolution fusion | flops 307494912 | bytes 5959680 | tf_op jit(solution)/shard_map/grqk,kgd->grqd/dot_general | solution.py:44
  147.0 1.7 %pad_maximum_fusion = bf16[3,96,4096]{2,1,0:T(8,128)(2,1)} fusion(bf16[1,96,4096]{2,1,0:T(8,128)(2,1)S(1)} %convert_element_type.78, bf16[1,96,4096]{2,1,0:T(8,128)(2,1)S(1)} %convert_element_type.75, bf16[1,96,4096]{2,1,0:T(8,128)(2,1)S(1)} %convert_element_type.72), kind=kLoop, calls=%fused_computation.28 | loop fusion | flops 2359296 | bytes 4718592 | tf_op jit(solution)/shard_map/concatenate | solution.py:157
  (69 shorter events, 12.4 us)
Async XLA Ops:
  0.0 9.6 %copy-start = (f32[2,64]{1,0:T(2,128)S(1)}, f32[2,64]{1,0:T(2,128)}, u32[]{:S(2)}) copy-start(f32[2,64]{1,0:T(2,128)} %param.12) | copy-start | bytes 1540
  0.0 29.8 %copy-start.4 = (bf16[3,96,4096]{2,1,0:T(8,128)(2,1)S(1)}, bf16[3,96,4096]{2,1,0:T(8,128)(2,1)}, u32[]{:S(2)}) copy-start(bf16[3,96,4096]{2,1,0:T(8,128)(2,1)} %param.7) | copy-start | bytes 7077892
  32.1 1.3 copy-start.10
  32.1 2.6 %copy-start.7 = (s32[3,96]{1,0:T(4,128)S(1)}, s32[3,96]{1,0:T(4,128)}, u32[]{:S(2)}) copy-start(s32[3,96]{1,0:T(4,128)} %param.11) | copy-start | bytes 3460
  44.3 4.8 %copy-start.6 = (bf16[3,96,512]{2,1,0:T(8,128)(2,1)S(1)}, bf16[3,96,512]{2,1,0:T(8,128)(2,1)}, u32[]{:S(2)}) copy-start(bf16[3,96,512]{2,1,0:T(8,128)(2,1)} %param.9) | copy-start | bytes 884740
  45.3 2.1 %copy-start.1 = (f32[4,384,96,8]{1,2,3,0:T(8,128)}, f32[4,384,96,8]{1,2,3,0:T(8,128)S(1)}, u32[]{:S(2)}) copy-start(f32[4,384,96,8]{1,2,3,0:T(8,128)S(1)} %get-tuple-element.33) | copy-start | bytes 14155780
  64.9 4.4 %copy-start.5 = (bf16[1,96,4,128]{3,2,1,0:T(4,128)(2,1)S(1)}, bf16[1,96,4,128]{3,2,1,0:T(4,128)(2,1)}, u32[]{:S(2)}) copy-start(bf16[1,96,4,128]{3,2,1,0:T(4,128)(2,1)} %get-tuple-element.17) | copy-start | bytes 294916
  64.9 19.1 %copy-start.9 = (s32[384]{0:T(512)S(1)}, s32[384]{0:T(512)}, u32[]{:S(2)}) copy-start(s32[384]{0:T(512)} %get-tuple-element.6) | copy-start | bytes 4612
  85.1 2.1 %copy-start.3 = (f32[4,384,96,8]{1,2,3,0:T(8,128)}, f32[4,384,96,8]{1,2,3,0:T(8,128)S(1)}, u32[]{:S(2)}) copy-start(f32[4,384,96,8]{1,2,3,0:T(8,128)S(1)} %get-tuple-element.31) | copy-start | bytes 14155780
  103.5 19.7 %copy-start.8 = (s32[384]{0:T(512)S(1)}, s32[384]{0:T(512)}, u32[]{:S(2)}) copy-start(s32[384]{0:T(512)} %get-tuple-element.5) | copy-start | bytes 4612
  124.4 2.1 %copy-start.2 = (f32[4,384,96,8]{1,2,3,0:T(8,128)}, f32[4,384,96,8]{1,2,3,0:T(8,128)S(1)}, u32[]{:S(2)}) copy-start(f32[4,384,96,8]{1,2,3,0:T(8,128)S(1)} %get-tuple-element.29) | copy-start | bytes 14155780
where the time goes:
time: 149 us
  blocking collectives  104 us (70%)
  matrix products  15.1 us (10%)
  local copies, waits for them, and re-layouts  14.5 us (10%)
  other arithmetic  14 us (9%)
    all_gather x3, blocking collectives, on_device(): lax.all_gather(key_rotated_rows, 'ctx', axis=1, tiled=True)  44.9 us
    all_gather x3, blocking collectives, on_device(): lax.all_gather(value_with_bias, 'ctx', axis=1, tiled=True)  43.8 us
    dot_general x3, matrix products, attend(): jnp.einsum('grqk,kgd->grqd', weights.astype(jnp.bfloat16), value_rows, pr...  11.1 us
    unnamed x1, blocking collectives  9.2 us
    unnamed x32, local copies, waits for them, and re-layouts  8.12 us
    all_gather x1, blocking collectives, on_device(): lax.all_gather(layer_bias, 'fsdp', axis=0, tiled=True).astype(jnp.float32)  6.2 us
    reduce_sum x3, other arithmetic, attend(): totals = jnp.sum(weights, axis=-1)  4.82 us
    dot_general x3, matrix products, attend(): jnp.einsum('qgrd,kgd->grqk', query_grouped, key_rows, preferred_element_t...  3.1 us

commit v1 on v0

--- a/solution.py
+++ b/solution.py
@@ -1,3 +1,4 @@
+import functools
 import math
 import jax
 import jax.numpy as jnp
@@ -9,6 +10,38 @@
 HEAD_SIZE = 128
 rope_base = 1000000.0
 masked_value = -1e30
+
+
+def arrange_plane_by_axis(local_values, mesh_dim):
+    local_next = lax.axis_size(mesh_dim)
+    r1 = lax.axis_index(mesh_dim)
+    finding, lower, item_now = (local_next, r1, local_values.shape[1])
+    current_value = jnp.zeros(
+        [dd * finding if dev_i == 1 else dd for dev_i, dd in enumerate(local_values.shape)],
+        local_values.dtype,
+    )
+    raw_out = lax.dynamic_update_slice_in_dim(current_value, local_values, lower * item_now, axis=1)
+    last = near = local_values
+    for w in range(1, finding // 2 + 1):
+        e_next = range(finding)
+        parts_out = map(lambda dev_i: (dev_i, (dev_i + 1) % finding), e_next)
+        value_now = list(parts_out)
+        last = lax.ppermute(last, mesh_dim, value_now)
+        raw_out = lax.dynamic_update_slice_in_dim(
+            raw_out, last, (lower - w) % finding * item_now, axis=1
+        )
+        if 2 * w < finding:
+            v_now = range(finding)
+            answer = map(lambda dev_i: (dev_i, (dev_i - 1) % finding), v_now)
+            block_now = list(answer)
+            near = lax.ppermute(near, mesh_dim, block_now)
+            raw_out = lax.dynamic_update_slice_in_dim(
+                raw_out, near, (lower + w) % finding * item_now, axis=1
+            )
+    return raw_out
+
+
+part_side = functools.partial(arrange_plane_by_axis, mesh_dim="ctx")
 
 
 def apply_rotation(states, positions, scale_factors):
@@ -148,7 +181,7 @@
             initial_state(key_heads_here, group_fraction, tokens_here),
             (
                 lax.all_gather(key_rotated_rows, "ctx", axis=1, tiled=True),
-                lax.all_gather(value_with_bias, "ctx", axis=1, tiled=True),
+                part_side(value_with_bias),
                 lax.all_gather(member_positions, "ctx", axis=1, tiled=True),
             ),
             jnp.int32(0),

time: 149 us -> 141 us (0.946)
  blocking collectives: 104 us -> 59.6 us
  starting transfers between devices: 0 us -> 12.6 us
  local copies, waits for them, and re-layouts: 14.5 us -> 26.1 us
  other arithmetic: 14 us -> 21.2 us
  matrix products: 15.1 us -> 19.6 us
    all_gather x3 -> x0, blocking collectives: 43.8 us -> none  [on_device(): lax.all_gather(value_with_bias, 'ctx', axis=1, tiled=True)]
    dynamic_update_slice x0 -> x12, local copies, waits for them, and re-layouts: none -> 16.3 us  [the longest x6 8.31 us: arrange_plane_by_axis(): lax.dynamic_update_slice_in_dim(raw_out, last, (lower - w) % finding * it...]
    ppermute x0 -> x9, starting transfers between devices: none -> 12.6 us  [the longest x3 7.4 us: arrange_plane_by_axis(): near = lax.ppermute(near, mesh_dim, block_now)]
    dot_general x3, matrix products: 3.1 us -> 8.37 us  [attend(): jnp.einsum('qgrd,kgd->grqk', query_grouped, key_rows, preferred_element_t...]
    unnamed x32 -> x44, local copies, waits for them, and re-layouts: 8.12 us -> 3.95 us
    concatenate x2, other arithmetic: 2.32 us -> 5.17 us  [apply_rotation(): jnp.concatenate([leading * cosine - trailing * sine_wave, trailing * cosi...]
    reduce_sum x3, other arithmetic: 4.82 us -> 7.15 us  [attend(): totals = jnp.sum(weights, axis=-1)]
    another operation x2, other arithmetic: 2.26 us -> 4.13 us
  transfers between devices with their start and end apart: 0 -> 9, of which waited for: 0 -> 0; matrix products, arithmetic and copies ran while one was open for 0% -> 40% of each run, Pallas kernels for 0% -> 0%
where the time goes in v1:
time: 141 us; the launch traced here: 140 us
  blocking collectives  59.6 us (42%)
  local copies, waits for them, and re-layouts  26.1 us (19%)
  other arithmetic  21.2 us (15%)
  matrix products  19.6 us (14%)
  starting transfers between devices  12.6 us (9%)
    all_gather x3, blocking collectives, on_device(): lax.all_gather(key_rotated_rows, 'ctx', axis=1, tiled=True)  44.8 us
    dot_general x3, matrix products, attend(): jnp.einsum('grqk,kgd->grqd', weights.astype(jnp.bfloat16), value_rows, pr...  11.1 us
    unnamed x1, blocking collectives  8.52 us
    dot_general x3, matrix products, attend(): jnp.einsum('qgrd,kgd->grqk', query_grouped, key_rows, preferred_element_t...  8.37 us
    dynamic_update_slice x6, local copies, waits for them, and re-layouts, arrange_plane_by_axis(): lax.dynamic_update_slice_in_dim(raw_out, last, (lower - w) % finding * it...  8.31 us
    ppermute x3, starting transfers between devices, arrange_plane_by_axis(): near = lax.ppermute(near, mesh_dim, block_now)  7.4 us
    reduce_sum x3, other arithmetic, attend(): totals = jnp.sum(weights, axis=-1)  7.15 us
    all_gather x1, blocking collectives, on_device(): lax.all_gather(layer_bias, 'fsdp', axis=0, tiled=True).astype(jnp.float32)  6.2 us
  transfers between devices with their start and end apart: 9, of which 0 were waited for; matrix products, arithmetic and copies ran while one was open for 40% of the time, Pallas kernels for 0%

profile of v1, /device:TPU:0, one launch (start us, length us, event | category | flops | bytes accessed | tf_op | source)
XLA Modules:
  0.0 140.4 jit_solution(15576002643564716948)
XLA Ops:
  0.7 6.2 %all-gather = bf16[4,1,2560]{2,1,0:T(2,128)(2,1)S(1)} all-gather(bf16[1,1,2560]{2,1,0:T(2,128)(2,1)S(1)} %reshape.188), channel_id=1, replica_groups=mesh['fsdp'=4,'ctx'=4,'uly'=2] {'fsdp'}, dimensions={0}, use_global_device_ids=true | all-gather | bytes 25600 | tf_op jit(solution)/shard_map/all_gather | solution.py:108
  9.1 2.0 %collective-permute-start = (bf16[1,96,512]{1,2,0:T(8,128)(2,1)}, bf16[1,96,512]{1,2,0:T(8,128)(2,1)}, u32[]{:S(2)}, u32[]{:S(2)}) collective-permute-start(bf16[1,96,512]{1,2,0:T(8,128)(2,1)} %bitcast.11), channel_id=1, source_target_pairs={{0,2},{2,4},{4,6},{6,0},{1,3},{3,5},{5,7},{7,1},{8,10},{10,12},{12... | collective-permute-start | bytes 294920 | tf_op jit(solution)/shard_map/ppermute | solution.py:29
  11.1 2.0 %collective-permute-start.1 = (bf16[1,96,512]{1,2,0:T(8,128)(2,1)}, bf16[1,96,512]{1,2,0:T(8,128)(2,1)}, u32[]{:S(2)}, u32[]{:S(2)}) collective-permute-start(bf16[1,96,512]{1,2,0:T(8,128)(2,1)} %bitcast.11), channel_id=1, source_target_pairs={{0,6},{2,0},{4,2},{6,4},{1,7},{3,1},{5,3},{7,5},{8,14},{10,8},{12,... | collective-permute-start | bytes 294920 | tf_op jit(solution)/shard_map/ppermute | solution.py:37
  13.2 3.8 %collective-permute-start.4 = (bf16[1,96,512]{1,2,0:T(8,128)(2,1)}, bf16[1,96,512]{1,2,0:T(8,128)(2,1)}, u32[]{:S(2)}, u32[]{:S(2)}) collective-permute-start(bf16[1,96,512]{1,2,0:T(8,128)(2,1)} %bitcast.21), channel_id=1, source_target_pairs={{0,6},{2,0},{4,2},{6,4},{1,7},{3,1},{5,3},{7,5},{8,14},{10,8},{12,... | collective-permute-start | bytes 294920 | tf_op jit(solution)/shard_map/ppermute | solution.py:37
  22.9 15.0 %all_gather.23 = bf16[1,384,512]{2,1,0:T(8,128)(2,1)S(1)} all-gather(bf16[1,96,512]{2,1,0:T(8,128)(2,1)S(1)} %slice.114), channel_id=1, replica_groups=mesh['fsdp'=4,'ctx'=4,'uly'=2] {'ctx'}, dimensions={1}, use_global_device_ids=true | all-gather | bytes 491520 | tf_op jit(solution)/shard_map/all_gather | solution.py:183
  39.1 3.6 %subtract_convert_fusion = (bf16[3,96,32,64]{3,1,2,0:T(8,128)(2,1)S(1)}, bf16[3,96,32,64]{3,1,2,0:T(8,128)(2,1)}) fusion(f32[3,96,32,128]{3,1,2,0:T(8,128)S(1)} %bitcast_add_fusion, f32[3,96,64]{2,1,0:T(8,128)S(1)} %copy-done.7, f32[3,96,64]{2,1,0:T(8,128)} %copy-done.5), kind=kLoop, calls=%fused_computation.18 | loop fusion | flops 4718592 | bytes 7225344 | tf_op jit(solution)/shard_map/convert.3
  44.4 4.1 %fusion.44 = (bf16[1,96,32,128]{3,1,2,0:T(8,128)(2,1)}, bf16[1,96,32,128]{3,1,2,0:T(8,128)(2,1)S(1)}, bf16[1,96,32,128]{3,1,2,0:T(8,128)(2,1)}) fusion(bf16[3,96,32,64]{3,1,2,0:T(8,128)(2,1)S(1)} %get-tuple-element.8, bf16[3,96,32,64]{3,1,2,0:T(8,128)(2,1)} %get-tuple-element.9), kind=kLoop, calls=%fused_computation.54 | loop fusion | flops 4718592 | bytes 4718592 | tf_op jit(solution)/shard_map/concatenate | solution.py:56
  48.5 8.5 %all-reduce.3 = (s32[384]{0:T(512)S(1)}, s32[384]{0:T(512)S(1)}, s32[384]{0:T(512)S(1)}) all-reduce(s32[384]{0:T(512)S(1)} %fusion.56, s32[384]{0:T(512)S(1)} %fusion.55, s32[384]{0:T(512)S(1)} %fusion.54), channel_id=1, replica_groups=mesh['fsdp'=4,'ctx'=4,'uly'=2] {'ctx'}, use_global_device_ids=true, to_apply=%add.2 | all-reduce | flops 1152 | bytes 9216
  57.8 4.2 %fusion.6 = (f32[4,8,96]{2,1,0:T(8,128)S(1)}, f32[4,384,96,8]{1,2,3,0:T(8,128)}) fusion(pred[96,384]{1,0:T(8,128)(4,1)S(1)} %broadcast_compare_fusion.2, bf16[384,4,128,1]{0,2,3,1:T(8,128)(2,1)S(1)} %bitcast.150, bf16[96,4,8,128]{3,0,2,1:T(8,128)(2,1)} %bitcast.147), kind=kOutput, calls=%fused_computation.13 | convolution fusion | flops 305525760 | bytes 5947392 | tf_op jit(solution)/shard_map/qgrd,kgd->grqk/dot_general | solution.py:68
  62.0 14.7 %all_gather.25 = bf16[1,384,512]{2,1,0:T(8,128)(2,1)S(1)} all-gather(bf16[1,96,512]{2,1,0:T(8,128)(2,1)S(1)} %slice.126), channel_id=1, replica_groups=mesh['fsdp'=4,'ctx'=4,'uly'=2] {'ctx'}, dimensions={1}, use_global_device_ids=true | all-gather | bytes 491520 | tf_op jit(solution)/shard_map/all_gather | solution.py:183
  77.1 3.2 %fusion.3 = (f32[4,8,96]{2,1,0:T(8,128)S(1)}, f32[4,384,96,8]{1,2,3,0:T(8,128)}) fusion(pred[96,384]{1,0:T(8,128)(4,1)S(1)} %broadcast_compare_fusion.1, bf16[384,4,128,1]{0,2,3,1:T(8,128)(2,1)S(1)} %bitcast.152, bf16[96,4,8,128]{3,0,2,1:T(8,128)(2,1)S(1)} %bitcast.146), kind=kOutput, calls=%fused_computation.8 | convolution fusion | flops 305525760 | bytes 5947392 | tf_op jit(solution)/shard_map/qgrd,kgd->grqk/dot_general | solution.py:68
  80.3 15.1 %all_gather.27 = bf16[1,384,512]{2,1,0:T(8,128)(2,1)S(1)} all-gather(bf16[1,96,512]{2,1,0:T(8,128)(2,1)S(1)} %slice.132), channel_id=1, replica_groups=mesh['fsdp'=4,'ctx'=4,'uly'=2] {'ctx'}, dimensions={1}, use_global_device_ids=true | all-gather | bytes 491520 | tf_op jit(solution)/shard_map/all_gather | solution.py:183
  95.6 3.4 %fusion.9 = f32[4,8,96]{2,1,0:T(8,128)S(1)} fusion(f32[4,384,96,8]{1,2,3,0:T(8,128)} %get-tuple-element.33, f32[4,8,96]{2,1,0:T(8,128)S(1)} %broadcast_maximum_fusion.2, pred[96,384]{1,0:T(8,128)(4,1)S(1)} %broadcast_compare_fusion.2), kind=kLoop, calls=%fused_computation.19 | loop fusion | flops 4715520 | bytes 4780032 | tf_op jit(solution)/shard_map/reduce_sum | solution.py:76
  104.2 2.2 %fusion.13 = f32[4,8,96]{2,1,0:T(8,128)} fusion(f32[4,384,96,8]{1,2,3,0:T(8,128)S(1)} %get-tuple-element.29, f32[4,8,96]{2,1,0:T(8,128)S(1)} %broadcast_maximum_fusion, pred[96,384]{1,0:T(8,128)(4,1)S(1)} %broadcast_compare_fusion), kind=kLoop, calls=%fused_computation.23 | loop fusion | flops 4715520 | bytes 4780032 | tf_op jit(solution)/shard_map/reduce_sum | solution.py:76
  110.3 1.6 %dynamic_update_slice.37 = bf16[1,384,512]{1,2,0:T(8,128)(2,1)S(1)} dynamic-update-slice(bf16[1,384,512]{1,2,0:T(8,128)(2,1)S(1)} %dynamic_update_slice.36, bf16[1,96,512]{1,2,0:T(8,128)(2,1)} %collective-permute-done, s32[]{:T(128)} %constant.60.clone.1, s32[]{:T(128)S(6)} %select_n.79, s32[]{:T(128)} %constant.60.clone.1) | dynamic-update-slice | bytes 196612 | tf_op jit(solution)/shard_map/dynamic_update_slice | solution.py:30
  112.0 1.6 %dynamic_update_slice.41 = bf16[1,384,512]{1,2,0:T(8,128)(2,1)S(1)} dynamic-update-slice(bf16[1,384,512]{1,2,0:T(8,128)(2,1)S(1)} %dynamic_update_slice.40, bf16[1,96,512]{1,2,0:T(8,128)(2,1)} %collective-permute-done.3, s32[]{:T(128)} %constant.60.clone.1, s32[]{:T(128)S(6)} %select_n.79, s32[]{:T(128)} %constant.60.clone.1) | dynamic-update-slice | bytes 196612 | tf_op jit(solution)/shard_map/dynamic_update_slice | solution.py:30
  115.8 2.1 %collective-permute-start.8 = (bf16[1,96,512]{1,2,0:T(8,128)(2,1)}, bf16[1,96,512]{1,2,0:T(8,128)(2,1)}, u32[]{:S(2)}, u32[]{:S(2)}) collective-permute-start(bf16[1,96,512]{1,2,0:T(8,128)(2,1)} %collective-permute-done.6), channel_id=1, source_target_pairs={{0,2},{2,4},{4,6},{6,0},{1,3},{3,5},{5,7},{7,1},{8,10},{10,12},{12... | collective-permute-start | bytes 294920 | tf_op jit(solution)/shard_map/ppermute | solution.py:29
  117.9 1.6 %dynamic_update_slice.38 = bf16[1,384,512]{1,2,0:T(8,128)(2,1)S(1)} dynamic-update-slice(bf16[1,384,512]{1,2,0:T(8,128)(2,1)S(1)} %dynamic_update_slice.37, bf16[1,96,512]{1,2,0:T(8,128)(2,1)} %collective-permute-done.1, s32[]{:T(128)} %constant.60.clone.1, s32[]{:T(128)S(6)} %select_n.81, s32[]{:T(128)} %constant.60.clone.1) | dynamic-update-slice | bytes 196612 | tf_op jit(solution)/shard_map/dynamic_update_slice | solution.py:38
  119.5 1.7 %dynamic_update_slice.42 = bf16[1,384,512]{1,2,0:T(8,128)(2,1)S(1)} dynamic-update-slice(bf16[1,384,512]{1,2,0:T(8,128)(2,1)S(1)} %dynamic_update_slice.41, bf16[1,96,512]{1,2,0:T(8,128)(2,1)} %collective-permute-done.4, s32[]{:T(128)} %constant.60.clone.1, s32[]{:T(128)S(6)} %select_n.81, s32[]{:T(128)} %constant.60.clone.1) | dynamic-update-slice | bytes 196612 | tf_op jit(solution)/shard_map/dynamic_update_slice | solution.py:38
  123.1 3.7 %fusion.35 = bf16[96,4,8,128]{3,0,2,1:T(8,128)(2,1)S(1)} fusion(bf16[384,4,128,1]{0,2,3,1:T(8,128)(2,1)S(1)} %bitcast.154, f32[4,384,96,8]{1,2,3,0:T(8,128)} %get-tuple-element.33, f32[4,8,96]{2,1,0:T(8,128)S(1)} %broadcast_maximum_fusion.2, pred[96,384]{1,0:T(8,128)(4,1)S(1)} %broadcast_compare_fusion.2, f32[96,4,8]{0,2,1:T(8,128)S(1)} %bitcast.160), kind=kOutput, calls=%fused_computation.50 | convolution fusion | flops 307494912 | bytes 5959680 | tf_op jit(solution)/shard_map/grqk,kgd->grqd/dot_general | solution.py:77
  127.7 3.7 %fusion.34 = bf16[96,4,8,128]{3,0,2,1:T(8,128)(2,1)S(1)} fusion(bf16[384,4,128,1]{0,2,3,1:T(8,128)(2,1)S(1)} %bitcast.155, f32[4,384,96,8]{1,2,3,0:T(8,128)} %get-tuple-element.31, f32[4,8,96]{2,1,0:T(8,128)S(1)} %broadcast_maximum_fusion.1, pred[96,384]{1,0:T(8,128)(4,1)S(1)} %broadcast_compare_fusion.1, f32[96,4,8]{0,2,1:T(8,128)S(1)} %bitcast.158), kind=kOutput, calls=%fused_computation.48 | convolution fusion | flops 307494912 | bytes 5959680 | tf_op jit(solution)/shard_map/grqk,kgd->grqd/dot_general | solution.py:77
  132.7 1.7 %dynamic_update_slice.47 = bf16[1,384,512]{1,2,0:T(8,128)(2,1)S(1)} dynamic-update-slice(bf16[1,384,512]{1,2,0:T(8,128)(2,1)S(1)} %dynamic_update_slice.46, bf16[1,96,512]{1,2,0:T(8,128)(2,1)} %collective-permute-done.8, s32[]{:T(128)} %constant.60.clone.1, s32[]{:T(128)S(6)} %select_n.83, s32[]{:T(128)} %constant.60.clone.1) | dynamic-update-slice | bytes 196612 | tf_op jit(solution)/shard_map/dynamic_update_slice | solution.py:30
  134.4 3.7 %fusion.33 = bf16[96,4,8,128]{3,0,2,1:T(8,128)(2,1)S(1)} fusion(bf16[384,4,128,1]{0,2,3,1:T(8,128)(2,1)S(1)} %bitcast.153, f32[4,384,96,8]{1,2,3,0:T(8,128)} %copy-done.2, f32[4,8,96]{2,1,0:T(8,128)} %copy-done.11, pred[96,384]{1,0:T(8,128)(4,1)} %copy-done.10, f32[96,4,8]{0,2,1:T(8,128)} %bitcast.159), kind=kOutput, calls=%fused_computation.46 | convolution fusion | flops 307494912 | bytes 5959680 | tf_op jit(solution)/shard_map/grqk,kgd->grqd/dot_general | solution.py:77
  138.7 1.7 %pad_maximum_fusion = bf16[3,96,4096]{2,1,0:T(8,128)(2,1)} fusion(bf16[1,96,4096]{2,1,0:T(8,128)(2,1)S(1)} %convert_element_type.78, bf16[1,96,4096]{2,1,0:T(8,128)(2,1)S(1)} %convert_element_type.75, bf16[1,96,4096]{2,1,0:T(8,128)(2,1)S(1)} %convert_element_type.72), kind=kLoop, calls=%fused_computation.28 | loop fusion | flops 2359296 | bytes 4718592 | tf_op jit(solution)/shard_map/concatenate | solution.py:190
  (105 shorter events, 28.0 us)
Async XLA Ops:
  0.0 20.3 %copy-start = (f32[2,64]{1,0:T(2,128)S(1)}, f32[2,64]{1,0:T(2,128)}, u32[]{:S(2)}) copy-start(f32[2,64]{1,0:T(2,128)} %param.12) | copy-start | bytes 1540
  0.0 20.3 %copy-start.15 = (s32[3]{0:T(128)S(1)}, s32[3]{0:T(128)}, u32[]{:S(2)}) copy-start(s32[3]{0:T(128)} %param.13) | copy-start | bytes 40
  8.1 30.1 %copy-start.4 = (bf16[3,96,4096]{2,1,0:T(8,128)(2,1)S(1)}, bf16[3,96,4096]{2,1,0:T(8,128)(2,1)}, u32[]{:S(2)}) copy-start(bf16[3,96,4096]{2,1,0:T(8,128)(2,1)} %param.7) | copy-start | bytes 7077892
  9.1 93.0 %collective-permute-start = (bf16[1,96,512]{1,2,0:T(8,128)(2,1)}, bf16[1,96,512]{1,2,0:T(8,128)(2,1)}, u32[]{:S(2)}, u32[]{:S(2)}) collective-permute-start(bf16[1,96,512]{1,2,0:T(8,128)(2,1)} %bitcast.11), channel_id=1, source_target_pairs={{0,2},{2,4},{4,6},{6,0},{1,3},{3,5},{5,7},{7,1},{8,10},{10,12},{12... | collective-permute-start | bytes 294920 | tf_op jit(solution)/shard_map/ppermute | solution.py:29
  11.1 104.6 %collective-permute-start.1 = (bf16[1,96,512]{1,2,0:T(8,128)(2,1)}, bf16[1,96,512]{1,2,0:T(8,128)(2,1)}, u32[]{:S(2)}, u32[]{:S(2)}) collective-permute-start(bf16[1,96,512]{1,2,0:T(8,128)(2,1)} %bitcast.11), channel_id=1, source_target_pairs={{0,6},{2,0},{4,2},{6,4},{1,7},{3,1},{5,3},{7,5},{8,14},{10,8},{12,... | collective-permute-start | bytes 294920 | tf_op jit(solution)/shard_map/ppermute | solution.py:37
  13.2 90.5 %collective-permute-start.3 = (bf16[1,96,512]{1,2,0:T(8,128)(2,1)}, bf16[1,96,512]{1,2,0:T(8,128)(2,1)}, u32[]{:S(2)}, u32[]{:S(2)}) collective-permute-start(bf16[1,96,512]{1,2,0:T(8,128)(2,1)} %bitcast.21), channel_id=1, source_target_pairs={{0,2},{2,4},{4,6},{6,0},{1,3},{3,5},{5,7},{7,1},{8,10},{10,12},{12... | collective-permute-start | bytes 294920 | tf_op jit(solution)/shard_map/ppermute | solution.py:29
  13.2 106.4 %collective-permute-start.4 = (bf16[1,96,512]{1,2,0:T(8,128)(2,1)}, bf16[1,96,512]{1,2,0:T(8,128)(2,1)}, u32[]{:S(2)}, u32[]{:S(2)}) collective-permute-start(bf16[1,96,512]{1,2,0:T(8,128)(2,1)} %bitcast.21), channel_id=1, source_target_pairs={{0,6},{2,0},{4,2},{6,4},{1,7},{3,1},{5,3},{7,5},{8,14},{10,8},{12,... | collective-permute-start | bytes 294920 | tf_op jit(solution)/shard_map/ppermute | solution.py:37
  17.0 96.6 %collective-permute-start.6 = (bf16[1,96,512]{1,2,0:T(8,128)(2,1)}, bf16[1,96,512]{1,2,0:T(8,128)(2,1)}, u32[]{:S(2)}, u32[]{:S(2)}) collective-permute-start(bf16[1,96,512]{1,2,0:T(8,128)(2,1)} %bitcast.31), channel_id=1, source_target_pairs={{0,2},{2,4},{4,6},{6,0},{1,3},{3,5},{5,7},{7,1},{8,10},{10,12},{12... | collective-permute-start | bytes 294920 | tf_op jit(solution)/shard_map/ppermute | solution.py:29
  38.2 0.9 copy-start.7
  39.1 3.6 %copy-start.16 = (u32[32]{0:T(128)S(1)}, u32[32]{0:T(128)}, u32[]{:S(2)}) copy-start(u32[32]{0:T(128)} %constant.86) | copy-start | bytes 388
  39.1 5.0 %copy-start.12 = (s32[3,96]{1,0:T(4,128)S(1)}, s32[3,96]{1,0:T(4,128)}, u32[]{:S(2)}) copy-start(s32[3,96]{1,0:T(4,128)} %param.11) | copy-start | bytes 3460
  48.5 13.5 %copy-start.9 = (bf16[1,96,4,128]{3,2,1,0:T(4,128)(2,1)S(1)}, bf16[1,96,4,128]{3,2,1,0:T(4,128)(2,1)}, u32[]{:S(2)}) copy-start(bf16[1,96,4,128]{3,2,1,0:T(4,128)(2,1)} %get-tuple-element.17) | copy-start | bytes 294916
  48.5 28.5 %copy-start.14 = (s32[96]{0:T(128)S(1)}, s32[96]{0:T(128)}, u32[]{:S(2)}) copy-start(s32[96]{0:T(128)} %get-tuple-element.27) | copy-start | bytes 1156
  48.5 28.6 %copy-start.3 = (bf16[1,96,32,128]{3,1,2,0:T(8,128)(2,1)S(1)}, bf16[1,96,32,128]{3,1,2,0:T(8,128)(2,1)}, u32[]{:S(2)}) copy-start(bf16[1,96,32,128]{3,1,2,0:T(8,128)(2,1)} %get-tuple-element.12) | copy-start | bytes 2359300
  61.9 18.3 %copy-start.8 = (bf16[1,96,4,128]{3,2,1,0:T(4,128)(2,1)S(1)}, bf16[1,96,4,128]{3,2,1,0:T(4,128)(2,1)}, u32[]{:S(2)}) copy-start(bf16[1,96,4,128]{3,2,1,0:T(4,128)(2,1)} %get-tuple-element.16) | copy-start | bytes 294916
  95.6 3.8 %copy-start.1 = (f32[4,384,96,8]{1,2,3,0:T(8,128)S(1)}, f32[4,384,96,8]{1,2,3,0:T(8,128)}, u32[]{:S(2)}) copy-start(f32[4,384,96,8]{1,2,3,0:T(8,128)} %get-tuple-element.31) | copy-start | bytes 14155780
  95.6 5.3 %copy-start.13 = (s32[96]{0:T(128)S(1)}, s32[96]{0:T(128)}, u32[]{:S(2)}) copy-start(s32[96]{0:T(128)} %get-tuple-element.26) | copy-start | bytes 1156
  101.0 5.4 %copy-start.10 = (pred[96,384]{1,0:T(8,128)(4,1)}, pred[96,384]{1,0:T(8,128)(4,1)S(1)}, u32[]{:S(2)}) copy-start(pred[96,384]{1,0:T(8,128)(4,1)S(1)} %broadcast_compare_fusion) | copy-start | bytes 110596
  102.1 2.2 %copy-start.2 = (f32[4,384,96,8]{1,2,3,0:T(8,128)}, f32[4,384,96,8]{1,2,3,0:T(8,128)S(1)}, u32[]{:S(2)}) copy-start(f32[4,384,96,8]{1,2,3,0:T(8,128)S(1)} %get-tuple-element.29) | copy-start | bytes 14155780
  102.1 11.5 %copy-start.11 = (f32[4,8,96]{2,1,0:T(8,128)}, f32[4,8,96]{2,1,0:T(8,128)S(1)}, u32[]{:S(2)}) copy-start(f32[4,8,96]{2,1,0:T(8,128)S(1)} %broadcast_maximum_fusion) | copy-start | bytes 36868
  102.1 19.1 %collective-permute-start.7 = (bf16[1,96,512]{1,2,0:T(8,128)(2,1)}, bf16[1,96,512]{1,2,0:T(8,128)(2,1)S(1)}, u32[]{:S(2)}, u32[]{:S(2)}) collective-permute-start(bf16[1,96,512]{1,2,0:T(8,128)(2,1)} %bitcast.31), channel_id=1, source_target_pairs={{0,6},{2,0},{4,2},{6,4},{1,7},{3,1},{5,3},{7,5},{8,14},{10,8},{12,... | collective-permute-start | bytes 294920 | tf_op jit(solution)/shard_map/ppermute | solution.py:37
  103.7 18.5 %collective-permute-start.2 = (bf16[1,96,512]{1,2,0:T(8,128)(2,1)}, bf16[1,96,512]{1,2,0:T(8,128)(2,1)S(1)}, u32[]{:S(2)}, u32[]{:S(2)}) collective-permute-start(bf16[1,96,512]{1,2,0:T(8,128)(2,1)} %collective-permute-done), channel_id=1, source_target_pairs={{0,2},{2,4},{4,6},{6,0},{1,3},{3,5},{5,7},{7,1},{8,10},{10,12},{12... | collective-permute-start | bytes 294920 | tf_op jit(solution)/shard_map/ppermute | solution.py:29
  113.6 13.2 %collective-permute-start.5 = (bf16[1,96,512]{1,2,0:T(8,128)(2,1)}, bf16[1,96,512]{1,2,0:T(8,128)(2,1)S(1)}, u32[]{:S(2)}, u32[]{:S(2)}) collective-permute-start(bf16[1,96,512]{1,2,0:T(8,128)(2,1)} %collective-permute-done.3), channel_id=1, source_target_pairs={{0,2},{2,4},{4,6},{6,0},{1,3},{3,5},{5,7},{7,1},{8,10},{10,12},{12... | collective-permute-start | bytes 294920 | tf_op jit(solution)/shard_map/ppermute | solution.py:29
  115.8 16.9 %collective-permute-start.8 = (bf16[1,96,512]{1,2,0:T(8,128)(2,1)}, bf16[1,96,512]{1,2,0:T(8,128)(2,1)}, u32[]{:S(2)}, u32[]{:S(2)}) collective-permute-start(bf16[1,96,512]{1,2,0:T(8,128)(2,1)} %collective-permute-done.6), channel_id=1, source_target_pairs={{0,2},{2,4},{4,6},{6,0},{1,3},{3,5},{5,7},{7,1},{8,10},{10,12},{12... | collective-permute-start | bytes 294920 | tf_op jit(solution)/shard_map/ppermute | solution.py:29
  (2 other events, 1.4 us)
